TPU v7x, 256 devices: a whole 4x4x8 slice. The times are simulated.
256 devices in a mesh: blk: 32 (over z_hi, y, core), head: 8 (over z_lo, x).
Axes of the slice: x: 4, y: 4, z: 8 (z_hi: 4, z_lo: 2; z = z_hi * 2 + z_lo), core: 2. Of those that a mesh axis runs over, the one named last changes fastest.
Arguments:
- query: bfloat16 [32768, 3072], P(('blk', 'head')), may hold values from -6 to 6
- keys: bfloat16 [32768, 3072], P(('blk', 'head')), may hold values from -6 to 6
- values: bfloat16 [32768, 3072], P(('blk', 'head')), may hold values from -6 to 6
- cotangent: bfloat16 [32768, 3072], P(('blk', 'head')), may hold values from -6 to 6
- kv_tiles: int32 [24, 256, 9], P('head'), may hold values from 0 to 255, as said below
Outputs:
- attended: bfloat16 [32768, 3072], P(('blk', 'head'))
- d_query: bfloat16 [32768, 3072], P(('blk', 'head'))
- d_keys: bfloat16 [32768, 3072], P(('blk', 'head'))
- d_values: bfloat16 [32768, 3072], P(('blk', 'head'))
Inputs may be any that keep to these rules, and one draw needn't show every extreme that they name: `kv_tiles`: the 9 entries of a row are distinct; the first 2 entries are the same in every row of one head (that head's global tiles); every other entry lies within 8 tiles of the row's query tile and is not a global tile of that head.
All inputs are finite; a program needn't handle non-finite values.
Results may differ from a plain program's by a relative error of at most 0.017.
Values may be sent and summed in bfloat16 or wider, within the bound.
A program may use at most 192 MiB of HBM per device.

v0:
```python
import jax
import jax.numpy as jnp
from jax import lax
from jax.sharding import PartitionSpec as P

HD = 128
TILE = 128
GLOBALS = 2
HALF = 8


def passed_along(block, axis, distance):
    devices = range(lax.axis_size(axis))
    route = [(i - distance, i) for i in devices if i - distance in devices]
    return lax.ppermute(block, axis, route)


def split_heads(field, count):
    heads = field.shape[1] // HD
    return field.reshape(count, TILE, heads, HD).transpose(2, 0, 1, 3)


def merge_heads(field):
    heads = field.shape[0]
    count = field.shape[1]
    return field.transpose(1, 2, 0, 3).reshape(count * TILE, heads * HD)


def recompute_probs(queries, chosen_keys, log_total):
    scale = HD ** (-0.5)
    scores = (
        jnp.einsum("tqd,tskd->tqsk", queries, chosen_keys, preferred_element_type=jnp.float32)
        * scale
    )
    return jnp.exp(scores - log_total)


def attend_forward(item):
    queries, pool_keys, pool_values, pool_index = item
    scale = HD ** (-0.5)
    chosen_keys = jnp.take(pool_keys, pool_index, axis=0)
    chosen_values = jnp.take(pool_values, pool_index, axis=0)
    scores = (
        jnp.einsum("tqd,tskd->tqsk", queries, chosen_keys, preferred_element_type=jnp.float32)
        * scale
    )
    peak = jnp.max(scores, axis=(2, 3), keepdims=True)
    log_total = peak + jnp.log(jnp.sum(jnp.exp(scores - peak), axis=(2, 3), keepdims=True))
    weights = jnp.exp(scores - log_total).astype(jnp.bfloat16)
    attended = jnp.einsum(
        "tqsk,tskd->tqd", weights, chosen_values, preferred_element_type=jnp.float32
    )
    return (attended.astype(jnp.bfloat16), log_total)


def attend_backward(item):
    queries, pool_keys, pool_values, grad_out, attended, log_total, pool_index = item
    scale = HD ** (-0.5)
    chosen_keys = jnp.take(pool_keys, pool_index, axis=0)
    chosen_values = jnp.take(pool_values, pool_index, axis=0)
    probs = recompute_probs(queries, chosen_keys, log_total)
    weights = probs.astype(jnp.bfloat16)
    delta = jnp.sum(grad_out.astype(jnp.float32) * attended.astype(jnp.float32), axis=-1)
    grad_probs = jnp.einsum(
        "tqd,tskd->tqsk", grad_out, chosen_values, preferred_element_type=jnp.float32
    )
    grad_scores = (probs * (grad_probs - delta[:, :, None, None])).astype(jnp.bfloat16)
    grad_query = (
        jnp.einsum("tqsk,tskd->tqd", grad_scores, chosen_keys, preferred_element_type=jnp.float32)
        * scale
    )
    key_slots = (
        jnp.einsum("tqsk,tqd->tskd", grad_scores, queries, preferred_element_type=jnp.float32)
        * scale
    )
    value_slots = jnp.einsum(
        "tqsk,tqd->tskd", weights, grad_out, preferred_element_type=jnp.float32
    )
    slot_count = pool_index.shape[0] * pool_index.shape[1]
    places = (
        pool_index.reshape(-1)[:, None] == jnp.arange(pool_keys.shape[0], dtype=jnp.int32)[None, :]
    ).astype(jnp.float32)
    key_pool = jnp.einsum(
        "sp,skd->pkd",
        places,
        key_slots.reshape(slot_count, TILE, HD),
        precision=lax.Precision.HIGHEST,
    )
    value_pool = jnp.einsum(
        "sp,skd->pkd",
        places,
        value_slots.reshape(slot_count, TILE, HD),
        precision=lax.Precision.HIGHEST,
    )
    return (grad_query.astype(jnp.bfloat16), key_pool, value_pool)


def per_device(query, keys, values, cotangent, kv_tiles):
    head_count = lax.axis_size("head")
    cycle_pos = lax.axis_index("blk")
    per_frame = query.shape[0] * head_count // TILE
    reach = -(-HALF // per_frame)
    span = (2 * reach + 1) * per_frame
    global_tiles = kv_tiles[:, 0, :GLOBALS]
    own_tiles = lax.dynamic_slice_in_dim(kv_tiles, cycle_pos * per_frame, per_frame, 1)
    moved = (
        lax.all_to_all(query, "head", split_axis=1, concat_axis=0, tiled=True),
        lax.all_to_all(keys, "head", split_axis=1, concat_axis=0, tiled=True),
        lax.all_to_all(values, "head", split_axis=1, concat_axis=0, tiled=True),
        lax.all_to_all(cotangent, "head", split_axis=1, concat_axis=0, tiled=True),
    )
    frame_keys = moved[1]
    frame_values = moved[2]
    offset = 1
    earlier = passed_along((frame_keys, frame_values), "blk", offset)
    later = passed_along((frame_keys, frame_values), "blk", -offset)
    earlier_keys = [earlier[0]]
    earlier_values = [earlier[1]]
    later_keys = [later[0]]
    later_values = [later[1]]
    near_keys = jnp.stack(earlier_keys[::-1] + later_keys, axis=0)
    near_values = jnp.stack(earlier_values[::-1] + later_values, axis=0)
    width = frame_keys.shape[1]
    all_keys = jnp.concatenate(
        [near_keys[:reach], frame_keys[None], near_keys[reach:]], axis=0
    ).reshape(span * TILE, width)
    all_values = jnp.concatenate(
        [near_values[:reach], frame_values[None], near_values[reach:]], axis=0
    ).reshape(span * TILE, width)
    own_keys = split_heads(frame_keys, per_frame)
    own_values = split_heads(frame_values, per_frame)
    tile_ids = cycle_pos * per_frame + jnp.arange(per_frame, dtype=jnp.int32)
    owner = global_tiles[:, :, None] == tile_ids[None, None, :]
    owner_mask = owner.astype(jnp.bfloat16)
    global_keys = jnp.einsum(
        "hjt,htkd->hjkd", owner_mask, own_keys, preferred_element_type=jnp.float32
    )
    global_values = jnp.einsum(
        "hjt,htkd->hjkd", owner_mask, own_values, preferred_element_type=jnp.float32
    )
    global_keys, global_values = (
        lax.psum(global_keys.astype(jnp.bfloat16), "blk").astype(jnp.float32),
        lax.psum(global_values.astype(jnp.bfloat16), "blk").astype(jnp.float32),
    )
    pool_keys = jnp.concatenate(
        [split_heads(all_keys, span), global_keys.astype(jnp.bfloat16)], axis=1
    )
    pool_values = jnp.concatenate(
        [split_heads(all_values, span), global_values.astype(jnp.bfloat16)], axis=1
    )
    relative = own_tiles - (cycle_pos - reach) * per_frame
    inside = (relative >= 0) & (relative < span)
    matches = own_tiles[:, :, :, None] == global_tiles[:, None, None, :]
    slot_numbers = jnp.arange(global_tiles.shape[1], dtype=jnp.int32)
    global_slot = jnp.sum(jnp.where(matches, slot_numbers[None, None, None, :], 0), axis=-1)
    pool_index = jnp.where(inside, relative, span + global_slot)
    queries = split_heads(moved[0], per_frame)
    grad_out = split_heads(moved[3], per_frame)
    attended, log_total = lax.map(attend_forward, (queries, pool_keys, pool_values, pool_index))
    grad_query, key_pool, value_pool = lax.map(
        attend_backward,
        (queries, pool_keys, pool_values, grad_out, attended, log_total, pool_index),
    )
    centre = reach * per_frame
    key_grad = key_pool[:, centre : centre + per_frame]
    value_grad = value_pool[:, centre : centre + per_frame]
    offset = 1
    lower = (reach - offset) * per_frame
    returned = (
        passed_along(
            key_pool[:, lower : lower + per_frame].astype(jnp.bfloat16), "blk", -offset
        ).astype(jnp.float32),
        passed_along(
            value_pool[:, lower : lower + per_frame].astype(jnp.bfloat16), "blk", -offset
        ).astype(jnp.float32),
    )
    key_grad = key_grad + returned[0]
    value_grad = value_grad + returned[1]
    upper = (reach + offset) * per_frame
    returned = (
        passed_along(
            key_pool[:, upper : upper + per_frame].astype(jnp.bfloat16), "blk", offset
        ).astype(jnp.float32),
        passed_along(
            value_pool[:, upper : upper + per_frame].astype(jnp.bfloat16), "blk", offset
        ).astype(jnp.float32),
    )
    key_grad = key_grad + returned[0]
    value_grad = value_grad + returned[1]
    summed = (
        lax.psum(key_pool[:, span:].astype(jnp.bfloat16), "blk").astype(jnp.float32),
        lax.psum(value_pool[:, span:].astype(jnp.bfloat16), "blk").astype(jnp.float32),
    )
    owner_float = owner.astype(jnp.float32)
    key_grad = key_grad + jnp.einsum(
        "hjt,hjkd->htkd", owner_float, summed[0], precision=lax.Precision.HIGHEST
    )
    value_grad = value_grad + jnp.einsum(
        "hjt,hjkd->htkd", owner_float, summed[1], precision=lax.Precision.HIGHEST
    )
    query_rows = merge_heads(grad_query)
    key_rows = merge_heads(key_grad.astype(jnp.bfloat16))
    value_rows = merge_heads(value_grad.astype(jnp.bfloat16))
    results = (
        lax.all_to_all(merge_heads(attended), "head", split_axis=0, concat_axis=1, tiled=True),
        lax.all_to_all(query_rows, "head", split_axis=0, concat_axis=1, tiled=True),
        lax.all_to_all(key_rows, "head", split_axis=0, concat_axis=1, tiled=True),
        lax.all_to_all(value_rows, "head", split_axis=0, concat_axis=1, tiled=True),
    )
    return (results[0], results[1], results[2], results[3])


def solution(mesh):
    placed = (
        P(("blk", "head"), None),
        P(("blk", "head"), None),
        P(("blk", "head"), None),
        P(("blk", "head"), None),
        P("head", None, None),
    )
    return jax.shard_map(
        per_device,
        mesh=mesh,
        in_specs=placed,
        out_specs=(
            P(("blk", "head"), None),
            P(("blk", "head"), None),
            P(("blk", "head"), None),
            P(("blk", "head"), None),
        ),
        check_vma=False,
    )
```

profile of v0, /device:TPU:160, one launch (start us, length us, event | category | flops | bytes accessed | tf_op | source)
XLA Modules:
  0.0 897.8 jit_solution(17046188124416074661)
XLA Ops:
  7.2 2.4 copy.91
  9.5 5.9 all-to-all-start.1
  16.6 10.3 %all-to-all-done.1 = bf16[128,8,384]{0,2,1:T(8,128)(2,1)S(1)} async-done(((bf16[128,8,384]{0,2,1:T(8,128)(2,1)}), bf16[128,8,384]{0,2,1:T(8,128)(2,1)S(1)}, u32[]{:S(2)}, u32[]{:S(2)}) %all-to-all-start.1) | async-done | bytes 786464 | tf_op jit(solution)/shard_map/all_to_all | solution.py:108
  26.9 4.2 all-to-all-start.2
  32.2 10.5 %all-to-all-done.2 = bf16[128,8,384]{0,2,1:T(8,128)(2,1)S(1)} async-done(((bf16[128,8,384]{0,2,1:T(8,128)(2,1)}), bf16[128,8,384]{0,2,1:T(8,128)(2,1)S(1)}, u32[]{:S(2)}, u32[]{:S(2)}) %all-to-all-start.2) | async-done | bytes 786464 | tf_op jit(solution)/shard_map/all_to_all | solution.py:109
  42.7 4.2 all-to-all-start
  47.4 4.0 collective-permute-start.3
  61.8 7.8 collective-permute-start.1
  72.8 6.1 all-to-all-start.4
  80.1 262.5 %all-reduce.7.cloned.1.call-done = (bf16[3,2,128,128]{3,1,2,0:T(2,128)(2,1)}, bf16[3,2,128,128]{3,1,2,0:T(2,128)(2,1)}) async-done(((bf16[3,2,128,128]{3,1,2,0:T(2,128)(2,1)}, bf16[3,2,128,128]{3,1,2,0:T(2,128)(2,1)}), (bf16[3,2,128,128]{3,1,2,0:T(2,128)(2,1)}, bf16[3,2,128,128]{3,1,2,0:T(2,128)(2,1)})) %all-reduce.7.cloned.1.call-update) | async-done | bytes 393232 | tf_op jit(solution)/shard_map/psum | solution.py:142
  345.5 3.1 pad_maximum_fusion.3
  348.6 5.9 reshape_reshape.7
  354.5 3.1 pad_maximum_fusion.1
  359.8 3.3 pad_maximum_fusion.2
  363.1 5.9 reshape_reshape.6
  373.4 32.2 %while.26 = (s32[]{:T(128)}, bf16[3,8,128,128]{3,2,1,0:T(8,128)(2,1)}, f32[3,8,128,1,1]{2,1,4,3,0:T(8,128)S(1)}, bf16[3,8,128,128]{3,2,1,0:T(8,128)(2,1)}, bf16[...) while((s32[]{:T(128)}, ...), condition=%wide.region_6.8_spmd, body=%wide.region_3.7_spmd.sunk | while | flops 615907776 | bytes 41720132 | solution.py:159
  375.0 2.4 gather_fusion
  385.7 2.4 gather_fusion
  396.5 2.4 gather_fusion
  407.9 5.7 all-to-all-start.3
  413.6 115.5 %while.27 = (s32[]{:T(128)}, bf16[3,8,128,128]{2,3,0,1:T(8,128)(2,1)}, f32[3,26,128,128]{3,1,2,0:T(8,128)}, f32[3,26,128,128]{3,1,2,0:T(8,128)}, bf16[3,8,128,12...) while((s32[]{:T(128)}, ...), condition=%wide.region_9.11_spmd, body=%wide.region_7.10_spmd.sunk | while | flops 2260996352 | bytes 105939144 | solution.py:160
  428.3 2.4 gather_fusion.2
  430.7 2.4 gather_fusion.3
  438.7 3.4 fusion.140
  443.1 8.2 bitcast_dynamic-update-slice_fusion.8
  453.2 6.0 bitcast_dynamic-update-slice_fusion.7
  463.2 2.4 gather_fusion.2
  465.7 2.4 gather_fusion.3
  473.7 3.4 fusion.140
  478.0 8.2 bitcast_dynamic-update-slice_fusion.8
  488.1 6.0 bitcast_dynamic-update-slice_fusion.7
  498.1 2.4 gather_fusion.2
  500.5 2.4 gather_fusion.3
  508.6 3.4 fusion.140
  512.9 8.2 bitcast_dynamic-update-slice_fusion.8
  523.0 6.0 bitcast_dynamic-update-slice_fusion.7
  529.0 3.5 convert.12
  532.6 5.7 all-to-all-start.5
  539.7 3.4 collective-permute-start.6
  545.8 3.6 convert.11
  550.2 279.6 %all-reduce.5.cloned.1.call-done = (bf16[3,2,128,128]{3,1,2,0:T(2,128)(2,1)}, bf16[3,2,128,128]{3,1,2,0:T(2,128)(2,1)}) async-done(((bf16[3,2,128,128]{3,1,2,0:T(2,128)(2,1)}, bf16[3,2,128,128]{3,1,2,0:T(2,128)(2,1)}), (bf16[3,2,128,128]{3,1,2,0:T(2,128)(2,1)}, bf16[3,2,128,128]{3,1,2,0:T(2,128)(2,1)})) %all-reduce.5.cloned.1.call-update) | async-done | bytes 393232 | tf_op jit(solution)/shard_map/psum | solution.py:191
  829.8 3.5 fusion.74
  833.3 2.4 copy.115
  835.7 5.8 all-to-all-start.7
  841.8 3.9 collective-permute-start.4
  847.7 13.1 %collective-permute-done.4 = bf16[3,8,128,128]{3,1,2,0:T(8,128)(2,1)S(1)} collective-permute-done((bf16[3,8,128,128]{3,1,2,0:T(8,128)(2,1)S(1)}, bf16[3,8,128,128]{3,1,2,0:T(8,128)(2,1)S(1)}, u32[]{:S(2)}, u32[]{:S(2)}) %collective-permute-start.4) | collective-permute-done | bytes 786464 | tf_op jit(solution)/shard_map/ppermute | solution.py:15
  860.8 11.0 %collective-permute-done.5 = bf16[3,8,128,128]{3,1,2,0:T(8,128)(2,1)S(1)} collective-permute-done((bf16[3,8,128,128]{3,1,2,0:T(8,128)(2,1)S(1)}, bf16[3,8,128,128]{3,1,2,0:T(8,128)(2,1)S(1)}, u32[]{:S(2)}, u32[]{:S(2)}) %collective-permute-start.5) | collective-permute-done | bytes 786464 | tf_op jit(solution)/shard_map/ppermute | solution.py:15
  875.2 5.7 all-to-all-start.6
  (181 shorter events, 111.8 us)
Async XLA Ops:
  7.2 8.3 copy-start.5
  9.5 21.5 %copy-start.6 = (bf16[128,3072]{1,0:T(8,128)(2,1)S(1)}, bf16[128,3072]{1,0:T(8,128)(2,1)}, u32[]{:S(2)}) copy-start(bf16[128,3072]{1,0:T(8,128)(2,1)} %param.11) | copy-start | bytes 2359300
  9.5 17.3 %all-to-all-start.1 = ((bf16[128,8,384]{0,2,1:T(8,128)(2,1)}), bf16[128,8,384]{0,2,1:T(8,128)(2,1)S(1)}, u32[]{:S(2)}, u32[]{:S(2)}) async-start(bf16[128,8,384]{0,2,1:T(8,128)(2,1)} %bitcast.39), calls=%async_computation.1 | async-start | bytes 1572864 | tf_op jit(solution)/shard_map/all_to_all | solution.py:108
  16.6 30.3 %copy-start.11 = (s32[3,256,9]{1,0,2:T(4,128)S(1)}, s32[3,256,9]{1,0,2:T(4,128)}, u32[]{:S(2)}) copy-start(s32[3,256,9]{1,0,2:T(4,128)} %param.15) | copy-start | bytes 82948
  26.9 15.8 %all-to-all-start.2 = ((bf16[128,8,384]{0,2,1:T(8,128)(2,1)}), bf16[128,8,384]{0,2,1:T(8,128)(2,1)S(1)}, u32[]{:S(2)}, u32[]{:S(2)}) async-start(bf16[128,8,384]{0,2,1:T(8,128)(2,1)} %bitcast.50), calls=%async_computation.2 | async-start | bytes 1572864 | tf_op jit(solution)/shard_map/all_to_all | solution.py:109
  42.7 30.2 %all-to-all-start = ((bf16[128,8,384]{0,2,1:T(8,128)(2,1)}), bf16[128,8,384]{0,2,1:T(8,128)(2,1)S(1)}, u32[]{:S(2)}, u32[]{:S(2)}) async-start(bf16[128,8,384]{0,2,1:T(8,128)(2,1)} %bitcast.35), calls=%async_computation | async-start | bytes 1572864 | tf_op jit(solution)/shard_map/all_to_all | solution.py:107
  46.9 295.8 %all-reduce.7.cloned.1.call-start = ((), (), s32[]{:S(2)}) async-start(), calls=%async_computation.9 | async-start | bytes 786432 | tf_op jit(solution)/shard_map/psum | solution.py:142
  47.0 13.6 %copy-start.9 = (s32[3,1,2]{2,0,1:T(4,128)}, s32[3,1,2]{2,0,1:T(4,128)S(1)}, u32[]{:S(2)}) copy-start(s32[3,1,2]{2,0,1:T(4,128)S(1)} %copy.129) | copy-start | bytes 76
  47.0 11.1 %copy-start.12 = (s32[8]{0:T(128)}, s32[8]{0:T(128)S(1)}, u32[]{:S(2)}) copy-start(s32[8]{0:T(128)S(1)} %iota_add_fusion) | copy-start | bytes 100
  47.4 298.2 %collective-permute-start.3 = (bf16[1024,384]{1,0:T(8,128)(2,1)S(1)}, bf16[1024,384]{1,0:T(8,128)(2,1)}, u32[]{:S(2)}, u32[]{:S(2)}) collective-permute-start(bf16[1024,384]{1,0:T(8,128)(2,1)S(1)} %bitcast.238), channel_id=1, source_target_pairs={{8,0},{16,8},{24,16},{32,24},{40,32},{48,40},{56,48},{64,56},{72,6... | collective-permute-start | bytes 2359304 | tf_op jit(solution)/shard_map/ppermute | solution.py:15
  51.3 294.2 %collective-permute-start.2 = (bf16[1024,384]{1,0:T(8,128)(2,1)S(1)}, bf16[1024,384]{1,0:T(8,128)(2,1)}, u32[]{:S(2)}, u32[]{:S(2)}) collective-permute-start(bf16[1024,384]{1,0:T(8,128)(2,1)S(1)} %bitcast.239), channel_id=1, source_target_pairs={{0,8},{8,16},{16,24},{24,32},{32,40},{40,48},{48,56},{56,64},{64,7... | collective-permute-start | bytes 2359304 | tf_op jit(solution)/shard_map/ppermute | solution.py:15
  58.1 13.6 %copy-start.7 = (bf16[128,3072]{1,0:T(8,128)(2,1)S(1)}, bf16[128,3072]{1,0:T(8,128)(2,1)}, u32[]{:S(2)}) copy-start(bf16[128,3072]{1,0:T(8,128)(2,1)} %param.14) | copy-start | bytes 2359300
  61.8 298.0 %collective-permute-start.1 = (bf16[1024,384]{1,0:T(8,128)(2,1)}, bf16[1024,384]{1,0:T(8,128)(2,1)}, u32[]{:S(2)}, u32[]{:S(2)}) collective-permute-start(bf16[1024,384]{1,0:T(8,128)(2,1)} %bitcast.41), channel_id=1, source_target_pairs={{8,0},{16,8},{24,16},{32,24},{40,32},{48,40},{56,48},{64,56},{72,6... | collective-permute-start | bytes 2359304 | tf_op jit(solution)/shard_map/ppermute | solution.py:15
  69.7 290.2 %collective-permute-start = (bf16[1024,384]{1,0:T(8,128)(2,1)}, bf16[1024,384]{1,0:T(8,128)(2,1)}, u32[]{:S(2)}, u32[]{:S(2)}) collective-permute-start(bf16[1024,384]{1,0:T(8,128)(2,1)} %bitcast.41), channel_id=1, source_target_pairs={{0,8},{8,16},{16,24},{24,32},{32,40},{40,48},{48,56},{56,64},{64,7... | collective-permute-start | bytes 2359304 | tf_op jit(solution)/shard_map/ppermute | solution.py:15
  72.8 335.0 %all-to-all-start.4 = ((bf16[128,8,384]{0,2,1:T(8,128)(2,1)}), bf16[128,8,384]{0,2,1:T(8,128)(2,1)}, u32[]{:S(2)}, u32[]{:S(2)}) async-start(bf16[128,8,384]{0,2,1:T(8,128)(2,1)} %bitcast.66), calls=%async_computation.4 | async-start | bytes 1572864 | tf_op jit(solution)/shard_map/all_to_all | solution.py:110
  380.3 1.7 copy-start.1
  391.0 1.7 copy-start.1
  401.7 1.7 copy-start.1
  407.9 124.7 %all-to-all-start.3 = ((bf16[8,128,384]{1,2,0:T(8,128)(2,1)}), bf16[8,128,384]{1,2,0:T(8,128)(2,1)}, u32[]{:S(2)}, u32[]{:S(2)}) async-start(bf16[8,128,384]{1,2,0:T(8,128)(2,1)} %bitcast.61), calls=%async_computation.3 | async-start | bytes 1572864 | tf_op jit(solution)/shard_map/all_to_all | solution.py:205
  430.7 2.4 copy-start
  433.1 2.0 copy-start.2
  437.3 1.4 copy-start.3
  443.1 8.2 copy-start.4
  465.6 2.4 copy-start
  468.1 2.1 copy-start.2
  472.3 1.4 copy-start.3
  478.0 8.2 copy-start.4
  500.5 2.4 copy-start
  502.9 2.1 copy-start.2
  507.1 1.4 copy-start.3
  512.9 8.2 copy-start.4
  532.6 303.1 %all-to-all-start.5 = ((bf16[8,128,384]{1,2,0:T(8,128)(2,1)}), bf16[8,128,384]{1,2,0:T(8,128)(2,1)}, u32[]{:S(2)}, u32[]{:S(2)}) async-start(bf16[8,128,384]{1,2,0:T(8,128)(2,1)} %bitcast.244), calls=%async_computation.5 | async-start | bytes 1572864 | tf_op jit(solution)/shard_map/all_to_all | solution.py:206
  538.3 291.5 %all-reduce.5.cloned.1.call-start = ((), (), s32[]{:S(2)}) async-start(), calls=%async_computation.8 | async-start | bytes 786432 | tf_op jit(solution)/shard_map/psum | solution.py:191
  539.7 290.1 %collective-permute-start.6 = (bf16[3,8,128,128]{3,1,2,0:T(8,128)(2,1)}, bf16[3,8,128,128]{3,1,2,0:T(8,128)(2,1)}, u32[]{:S(2)}, u32[]{:S(2)}) collective-permute-start(bf16[3,8,128,128]{3,1,2,0:T(8,128)(2,1)} %get-tuple-element.225), channel_id=1, source_target_pairs={{8,0},{16,8},{24,16},{32,24},{40,32},{48,40},{56,48},{64,56},{72,6... | collective-permute-start | bytes 2359304 | tf_op jit(solution)/shard_map/ppermute | solution.py:15
  543.1 286.7 %collective-permute-start.7 = (bf16[3,8,128,128]{3,1,2,0:T(8,128)(2,1)}, bf16[3,8,128,128]{3,1,2,0:T(8,128)(2,1)}, u32[]{:S(2)}, u32[]{:S(2)}) collective-permute-start(bf16[3,8,128,128]{3,1,2,0:T(8,128)(2,1)} %get-tuple-element.226), channel_id=1, source_target_pairs={{0,8},{8,16},{16,24},{24,32},{32,40},{40,48},{48,56},{56,64},{64,7... | collective-permute-start | bytes 2359304 | tf_op jit(solution)/shard_map/ppermute | solution.py:15
  545.8 284.0 %copy-start.10 = (s32[3,1,2]{2,0,1:T(4,128)S(1)}, s32[3,1,2]{2,0,1:T(4,128)}, u32[]{:S(2)}) copy-start(s32[3,1,2]{2,0,1:T(4,128)} %copy-done.9) | copy-start | bytes 76
  545.8 284.0 %copy-start.13 = (s32[8]{0:T(128)S(1)}, s32[8]{0:T(128)}, u32[]{:S(2)}) copy-start(s32[8]{0:T(128)} %copy-done.12) | copy-start | bytes 100
  835.7 36.1 %copy-start.8 = (bf16[3,2,128,128]{3,1,2,0:T(2,128)(2,1)S(1)}, bf16[3,2,128,128]{3,1,2,0:T(2,128)(2,1)}, u32[]{:S(2)}) copy-start(bf16[3,2,128,128]{3,1,2,0:T(2,128)(2,1)} %get-tuple-element.209) | copy-start | bytes 589828
  835.7 39.6 %all-to-all-start.7 = ((bf16[8,128,384]{1,2,0:T(8,128)(2,1)}), bf16[8,128,384]{1,2,0:T(8,128)(2,1)}, u32[]{:S(2)}, u32[]{:S(2)}) async-start(bf16[8,128,384]{1,2,0:T(8,128)(2,1)} %bitcast.242), calls=%async_computation.7 | async-start | bytes 1572864 | tf_op jit(solution)/shard_map/all_to_all | solution.py:208
  841.8 19.0 %collective-permute-start.4 = (bf16[3,8,128,128]{3,1,2,0:T(8,128)(2,1)S(1)}, bf16[3,8,128,128]{3,1,2,0:T(8,128)(2,1)S(1)}, u32[]{:S(2)}, u32[]{:S(2)}) collective-permute-start(bf16[3,8,128,128]{3,1,2,0:T(8,128)(2,1)S(1)} %get-tuple-element.227), channel_id=1, source_target_pairs={{8,0},{16,8},{24,16},{32,24},{40,32},{48,40},{56,48},{64,56},{72,6... | collective-permute-start | bytes 2359304 | tf_op jit(solution)/shard_map/ppermute | solution.py:15
  845.7 26.1 %collective-permute-start.5 = (bf16[3,8,128,128]{3,1,2,0:T(8,128)(2,1)S(1)}, bf16[3,8,128,128]{3,1,2,0:T(8,128)(2,1)S(1)}, u32[]{:S(2)}, u32[]{:S(2)}) collective-permute-start(bf16[3,8,128,128]{3,1,2,0:T(8,128)(2,1)S(1)} %get-tuple-element.228), channel_id=1, source_target_pairs={{0,8},{8,16},{16,24},{24,32},{32,40},{40,48},{48,56},{56,64},{64,7... | collective-permute-start | bytes 2359304 | tf_op jit(solution)/shard_map/ppermute | solution.py:15
  875.2 14.3 %all-to-all-start.6 = ((bf16[8,128,384]{1,2,0:T(8,128)(2,1)}), bf16[8,128,384]{1,2,0:T(8,128)(2,1)S(1)}, u32[]{:S(2)}, u32[]{:S(2)}) async-start(bf16[8,128,384]{1,2,0:T(8,128)(2,1)} %bitcast.75), calls=%async_computation.6 | async-start | bytes 1572864 | tf_op jit(solution)/shard_map/all_to_all | solution.py:207
Sparse Core Ops, SparseCore 0:
  60.5 282.0 all-reduce.6
  550.3 279.4 all-reduce.4
where the time goes:
time: 904 us; the launch traced here: 898 us
  waiting for transfers between devices  589 us (65%)
  matrix products  95.7 us (11%)
  local copies, waits for them, and re-layouts  92.7 us (10%)
  starting transfers between devices  70.2 us (8%)
  other arithmetic  24.9 us (3%)
  between operations  14.5 us (2%)
  loops' own time  11 us (1%)
    psum x1, waiting for transfers between devices, per_device(): lax.psum(key_pool[:, span:].astype(jnp.bfloat16), 'blk').astype(jnp.float32)  280 us
    psum x1, waiting for transfers between devices, per_device(): lax.psum(global_keys.astype(jnp.bfloat16), 'blk').astype(jnp.float32)  262 us
    ppermute x8, starting transfers between devices, passed_along(): return lax.ppermute(block, axis, route)  26.8 us
    dot_general x3, matrix products, attend_backward(): jnp.einsum('sp,skd->pkd', places, value_slots.reshape(slot_count, TILE, H...  24.7 us
    ppermute x8, waiting for transfers between devices, passed_along(): return lax.ppermute(block, axis, route)  24.1 us
  transfers between devices with their start and end apart: 18, of which 7 were waited for; matrix products, arithmetic and copies ran while one was open for 23% of the time, Pallas kernels for 0%

commit v1 on v0

--- a/solution.py
+++ b/solution.py
@@ -7,6 +7,11 @@
 TILE = 128
 GLOBALS = 2
 HALF = 8
+
+
+def place_the_heads(arr):
+    out_arr = jnp.sum(jax.lax.all_gather(arr, "blk"), axis=0)
+    return out_arr
 
 
 def passed_along(block, axis, distance):
@@ -188,7 +193,7 @@
     key_grad = key_grad + returned[0]
     value_grad = value_grad + returned[1]
     summed = (
-        lax.psum(key_pool[:, span:].astype(jnp.bfloat16), "blk").astype(jnp.float32),
+        place_the_heads(key_pool[:, span:].astype(jnp.bfloat16)).astype(jnp.float32),
         lax.psum(value_pool[:, span:].astype(jnp.bfloat16), "blk").astype(jnp.float32),
     )
     owner_float = owner.astype(jnp.float32)

time: 904 us -> 939 us (1.039)
  blocking collectives: 0 us -> 14.4 us
  waiting for transfers between devices: 589 us -> 602 us
    all_gather x0 -> x1, waiting for transfers between devices: none -> 61.5 us  [place_the_heads(): out_arr = jnp.sum(jax.lax.all_gather(arr, 'blk'), axis=0)]
    psum x1, waiting for transfers between devices: 280 us -> 251 us  [per_device(): lax.psum(value_pool[:, span:].astype(jnp.bfloat16), 'blk')]
    ppermute x8, waiting for transfers between devices: 24.1 us -> 0.02 us  [passed_along(): return lax.ppermute(block, axis, route)]
    all_to_all x0 -> x1, blocking collectives: none -> 14.4 us  [per_device(): lax.all_to_all(merge_heads(attended), 'head', split_axis=0, concat_axis=1...]
  transfers between devices with their start and end apart: 18 -> 18, of which waited for: 7 -> 6; matrix products, arithmetic and copies ran while one was open for 23% -> 11% of each run, Pallas kernels for 0% -> 0%
where the time goes in v1:
time: 939 us; the launch traced here: 929 us
  waiting for transfers between devices  602 us (64%)
  local copies, waits for them, and re-layouts  95.7 us (10%)
  matrix products  95.6 us (10%)
  starting transfers between devices  66.7 us (7%)
  other arithmetic  29.1 us (3%)
  blocking collectives  14.4 us (2%)
  between operations  14.2 us (2%)
  loops' own time  11 us (1%)
    psum x1, waiting for transfers between devices, per_device(): lax.psum(global_keys.astype(jnp.bfloat16), 'blk').astype(jnp.float32)  263 us
    psum x1, waiting for transfers between devices, per_device(): lax.psum(value_pool[:, span:].astype(jnp.bfloat16), 'blk')  251 us
    all_gather x1, waiting for transfers between devices, place_the_heads(): out_arr = jnp.sum(jax.lax.all_gather(arr, 'blk'), axis=0)  61.5 us
    ppermute x8, starting transfers between devices, passed_along(): return lax.ppermute(block, axis, route)  29.2 us
    dot_general x3, matrix products, attend_backward(): jnp.einsum('sp,skd->pkd', places, value_slots.reshape(slot_count, TILE, H...  24.6 us
  transfers between devices with their start and end apart: 18, of which 6 were waited for; matrix products, arithmetic and copies ran while one was open for 11% of the time, Pallas kernels for 0%

profile of v1, /device:TPU:160, one launch (start us, length us, event | category | flops | bytes accessed | tf_op | source)
XLA Modules:
  0.0 929.1 jit_solution(6384496035808193703)
XLA Ops:
  9.5 5.9 all-to-all-start.1
  16.6 10.3 %all-to-all-done.1 = bf16[128,8,384]{0,2,1:T(8,128)(2,1)S(1)} async-done(((bf16[128,8,384]{0,2,1:T(8,128)(2,1)}), bf16[128,8,384]{0,2,1:T(8,128)(2,1)S(1)}, u32[]{:S(2)}, u32[]{:S(2)}) %all-to-all-start.1) | async-done | bytes 786464 | tf_op jit(solution)/shard_map/all_to_all | solution.py:113
  26.9 4.2 all-to-all-start.2
  32.2 10.5 %all-to-all-done.2 = bf16[128,8,384]{0,2,1:T(8,128)(2,1)S(1)} async-done(((bf16[128,8,384]{0,2,1:T(8,128)(2,1)}), bf16[128,8,384]{0,2,1:T(8,128)(2,1)S(1)}, u32[]{:S(2)}, u32[]{:S(2)}) %all-to-all-start.2) | async-done | bytes 786464 | tf_op jit(solution)/shard_map/all_to_all | solution.py:114
  42.7 4.2 all-to-all-start
  47.4 4.0 collective-permute-start.3
  61.8 7.8 collective-permute-start.1
  72.8 5.7 all-to-all-start.4
  80.1 262.5 %all-reduce.6.cloned.1.call-done = (bf16[3,2,128,128]{3,1,2,0:T(2,128)(2,1)}, bf16[3,2,128,128]{3,1,2,0:T(2,128)(2,1)}) async-done(((bf16[3,2,128,128]{3,1,2,0:T(2,128)(2,1)}, bf16[3,2,128,128]{3,1,2,0:T(2,128)(2,1)}), (bf16[3,2,128,128]{3,1,2,0:T(2,128)(2,1)}, bf16[3,2,128,128]{3,1,2,0:T(2,128)(2,1)})) %all-reduce.6.cloned.1.call-update) | async-done | bytes 393232 | tf_op jit(solution)/shard_map/psum | solution.py:147
  345.5 3.1 pad_maximum_fusion.3
  348.6 5.9 reshape_reshape.7
  354.5 3.1 pad_maximum_fusion.1
  359.8 3.3 pad_maximum_fusion.2
  363.1 5.9 reshape_reshape.6
  373.4 32.2 %while.26 = (s32[]{:T(128)}, bf16[3,8,128,128]{3,2,1,0:T(8,128)(2,1)}, f32[3,8,128,1,1]{2,1,4,3,0:T(8,128)S(1)}, bf16[3,8,128,128]{3,2,1,0:T(8,128)(2,1)}, bf16[...) while((s32[]{:T(128)}, ...), condition=%wide.region_6.8_spmd, body=%wide.region_3.7_spmd.sunk | while | flops 615907776 | bytes 41720132 | solution.py:164
  375.0 2.4 gather_fusion
  385.8 2.4 gather_fusion
  396.5 2.4 gather_fusion
  405.6 115.5 %while.27 = (s32[]{:T(128)}, bf16[3,8,128,128]{2,3,0,1:T(8,128)(2,1)}, f32[3,26,128,128]{3,1,2,0:T(8,128)}, f32[3,26,128,128]{3,1,2,0:T(8,128)}, bf16[3,8,128,12...) while((s32[]{:T(128)}, ...), condition=%wide.region_9.11_spmd, body=%wide.region_7.10_spmd.sunk | while | flops 2260996352 | bytes 105939144 | solution.py:165
  420.4 2.4 gather_fusion.2
  422.8 2.4 gather_fusion.3
  430.8 3.4 fusion.140
  435.2 8.2 bitcast_dynamic-update-slice_fusion.8
  445.3 6.0 bitcast_dynamic-update-slice_fusion.7
  455.3 2.4 gather_fusion.2
  457.7 2.4 gather_fusion.3
  465.7 3.4 fusion.140
  470.1 8.2 bitcast_dynamic-update-slice_fusion.8
  480.2 6.0 bitcast_dynamic-update-slice_fusion.7
  490.2 2.4 gather_fusion.2
  500.7 3.4 fusion.140
  505.0 8.2 bitcast_dynamic-update-slice_fusion.8
  515.1 6.0 bitcast_dynamic-update-slice_fusion.7
  521.1 3.5 convert.13
  527.2 3.5 convert.12
  533.9 14.4 %all_to_all.146 = bf16[8,128,384]{1,2,0:T(8,128)(2,1)} all-to-all(bf16[8,128,384]{1,2,0:T(8,128)(2,1)} %bitcast.244), channel_id=1, replica_groups=mesh['blk'=32,'head'=8] {'head'}, dimensions={0} | all-to-all | bytes 1572864 | tf_op jit(solution)/shard_map/all_to_all | solution.py:210
  548.3 5.7 all-to-all-start.5
  554.1 2.6 fusion.100
  556.7 5.7 collective-permute-start.6
  564.4 251.3 %all-reduce.4.cloned.1.call-done = bf16[3,2,128,128]{3,1,2,0:T(2,128)(2,1)} async-done(((bf16[3,2,128,128]{3,1,2,0:T(2,128)(2,1)}), bf16[3,2,128,128]{3,1,2,0:T(2,128)(2,1)}) %all-reduce.4.cloned.1.call-update) | async-done | bytes 196624 | tf_op jit(solution)/shard_map/psum | solution.py:197
  815.7 3.5 fusion.74
  819.2 2.4 copy.190
  821.6 5.7 all-to-all-start.7
  828.7 3.9 collective-permute-start.4
  834.6 61.5 %all-gather.3.cloned.1.call-done = bf16[96,2,128,128]{3,2,1,0:T(8,128)(2,1)} async-done(((bf16[3,2,128,128]{3,2,1,0:T(8,128)(2,1)}), bf16[96,2,128,128]{3,2,1,0:T(8,128)(2,1)}) %all-gather.3.cloned.1.call-update) | async-done | bytes 6291472 | tf_op jit(solution)/shard_map/all_gather | solution.py:13
  896.0 4.2 reduce_sum.40
  903.7 5.6 all-to-all-start.6
  915.1 6.1 all-to-all-done.6
  (187 shorter events, 115.5 us)
Async XLA Ops:
  7.2 8.3 copy-start.7
  9.5 21.5 %copy-start.8 = (bf16[128,3072]{1,0:T(8,128)(2,1)S(1)}, bf16[128,3072]{1,0:T(8,128)(2,1)}, u32[]{:S(2)}) copy-start(bf16[128,3072]{1,0:T(8,128)(2,1)} %param.11) | copy-start | bytes 2359300
  9.5 17.3 %all-to-all-start.1 = ((bf16[128,8,384]{0,2,1:T(8,128)(2,1)}), bf16[128,8,384]{0,2,1:T(8,128)(2,1)S(1)}, u32[]{:S(2)}, u32[]{:S(2)}) async-start(bf16[128,8,384]{0,2,1:T(8,128)(2,1)} %bitcast.39), calls=%async_computation.1 | async-start | bytes 1572864 | tf_op jit(solution)/shard_map/all_to_all | solution.py:113
  16.6 30.3 %copy-start.12 = (s32[3,256,9]{1,0,2:T(4,128)S(1)}, s32[3,256,9]{1,0,2:T(4,128)}, u32[]{:S(2)}) copy-start(s32[3,256,9]{1,0,2:T(4,128)} %param.15) | copy-start | bytes 82948
  26.9 15.8 %all-to-all-start.2 = ((bf16[128,8,384]{0,2,1:T(8,128)(2,1)}), bf16[128,8,384]{0,2,1:T(8,128)(2,1)S(1)}, u32[]{:S(2)}, u32[]{:S(2)}) async-start(bf16[128,8,384]{0,2,1:T(8,128)(2,1)} %bitcast.50), calls=%async_computation.2 | async-start | bytes 1572864 | tf_op jit(solution)/shard_map/all_to_all | solution.py:114
  42.7 30.2 %all-to-all-start = ((bf16[128,8,384]{0,2,1:T(8,128)(2,1)}), bf16[128,8,384]{0,2,1:T(8,128)(2,1)S(1)}, u32[]{:S(2)}, u32[]{:S(2)}) async-start(bf16[128,8,384]{0,2,1:T(8,128)(2,1)} %bitcast.35), calls=%async_computation | async-start | bytes 1572864 | tf_op jit(solution)/shard_map/all_to_all | solution.py:112
  46.9 295.7 %all-reduce.6.cloned.1.call-start = ((), (), s32[]{:S(2)}) async-start(), calls=%async_computation.10 | async-start | bytes 786432 | tf_op jit(solution)/shard_map/psum | solution.py:147
  47.0 13.6 %copy-start.10 = (s32[3,1,2]{2,0,1:T(4,128)}, s32[3,1,2]{2,0,1:T(4,128)S(1)}, u32[]{:S(2)}) copy-start(s32[3,1,2]{2,0,1:T(4,128)S(1)} %copy.204) | copy-start | bytes 76
  47.0 11.1 %copy-start.13 = (s32[8]{0:T(128)}, s32[8]{0:T(128)S(1)}, u32[]{:S(2)}) copy-start(s32[8]{0:T(128)S(1)} %iota_add_fusion) | copy-start | bytes 100
  47.4 298.2 %collective-permute-start.3 = (bf16[1024,384]{1,0:T(8,128)(2,1)S(1)}, bf16[1024,384]{1,0:T(8,128)(2,1)}, u32[]{:S(2)}, u32[]{:S(2)}) collective-permute-start(bf16[1024,384]{1,0:T(8,128)(2,1)S(1)} %bitcast.237), channel_id=1, source_target_pairs={{8,0},{16,8},{24,16},{32,24},{40,32},{48,40},{56,48},{64,56},{72,6... | collective-permute-start | bytes 2359304 | tf_op jit(solution)/shard_map/ppermute | solution.py:20
  51.3 294.2 %collective-permute-start.2 = (bf16[1024,384]{1,0:T(8,128)(2,1)S(1)}, bf16[1024,384]{1,0:T(8,128)(2,1)}, u32[]{:S(2)}, u32[]{:S(2)}) collective-permute-start(bf16[1024,384]{1,0:T(8,128)(2,1)S(1)} %bitcast.238), channel_id=1, source_target_pairs={{0,8},{8,16},{16,24},{24,32},{32,40},{40,48},{48,56},{56,64},{64,7... | collective-permute-start | bytes 2359304 | tf_op jit(solution)/shard_map/ppermute | solution.py:20
  58.1 13.6 %copy-start.9 = (bf16[128,3072]{1,0:T(8,128)(2,1)S(1)}, bf16[128,3072]{1,0:T(8,128)(2,1)}, u32[]{:S(2)}) copy-start(bf16[128,3072]{1,0:T(8,128)(2,1)} %param.14) | copy-start | bytes 2359300
  61.8 298.0 %collective-permute-start.1 = (bf16[1024,384]{1,0:T(8,128)(2,1)}, bf16[1024,384]{1,0:T(8,128)(2,1)}, u32[]{:S(2)}, u32[]{:S(2)}) collective-permute-start(bf16[1024,384]{1,0:T(8,128)(2,1)} %bitcast.41), channel_id=1, source_target_pairs={{8,0},{16,8},{24,16},{32,24},{40,32},{48,40},{56,48},{64,56},{72,6... | collective-permute-start | bytes 2359304 | tf_op jit(solution)/shard_map/ppermute | solution.py:20
  69.7 290.1 %collective-permute-start = (bf16[1024,384]{1,0:T(8,128)(2,1)}, bf16[1024,384]{1,0:T(8,128)(2,1)}, u32[]{:S(2)}, u32[]{:S(2)}) collective-permute-start(bf16[1024,384]{1,0:T(8,128)(2,1)} %bitcast.41), channel_id=1, source_target_pairs={{0,8},{8,16},{16,24},{24,32},{32,40},{40,48},{48,56},{56,64},{64,7... | collective-permute-start | bytes 2359304 | tf_op jit(solution)/shard_map/ppermute | solution.py:20
  72.8 332.8 %all-to-all-start.4 = ((bf16[128,8,384]{0,2,1:T(8,128)(2,1)}), bf16[128,8,384]{0,2,1:T(8,128)(2,1)}, u32[]{:S(2)}, u32[]{:S(2)}) async-start(bf16[128,8,384]{0,2,1:T(8,128)(2,1)} %bitcast.66), calls=%async_computation.4 | async-start | bytes 1572864 | tf_op jit(solution)/shard_map/all_to_all | solution.py:115
  78.5 737.2 %all-reduce.4.cloned.1.call-start = ((), (), s32[]{:S(2)}) async-start(), calls=%async_computation.8 | async-start | bytes 393216 | tf_op jit(solution)/shard_map/psum | solution.py:197
  380.3 1.7 copy-start.1
  391.0 1.7 copy-start.1
  401.8 1.7 copy-start.1
  422.8 2.4 copy-start
  425.2 2.0 copy-start.2
  429.4 1.4 copy-start.3
  435.2 8.2 copy-start.4
  457.7 2.4 copy-start
  460.1 2.0 copy-start.2
  464.3 1.4 copy-start.3
  470.1 8.2 copy-start.4
  492.6 2.4 copy-start
  495.0 2.1 copy-start.2
  499.2 1.4 copy-start.3
  505.0 8.2 copy-start.4
  524.6 1.7 copy-start.5
  527.1 368.9 %all-gather.3.cloned.1.call-start = ((), (), s32[]{:S(2)}) async-start(), calls=%async_computation.9 | async-start | bytes 6488064 | tf_op jit(solution)/shard_map/all_gather | solution.py:13
  548.3 267.4 %copy-start.11 = (s32[3,1,2]{2,0,1:T(4,128)S(1)}, s32[3,1,2]{2,0,1:T(4,128)}, u32[]{:S(2)}) copy-start(s32[3,1,2]{2,0,1:T(4,128)} %copy-done.10) | copy-start | bytes 76
  548.3 267.4 %copy-start.14 = (s32[8]{0:T(128)S(1)}, s32[8]{0:T(128)}, u32[]{:S(2)}) copy-start(s32[8]{0:T(128)} %copy-done.13) | copy-start | bytes 100
  548.3 273.3 %all-to-all-start.5 = ((bf16[8,128,384]{1,2,0:T(8,128)(2,1)}), bf16[8,128,384]{1,2,0:T(8,128)(2,1)}, u32[]{:S(2)}, u32[]{:S(2)}) async-start(bf16[8,128,384]{1,2,0:T(8,128)(2,1)} %bitcast.245), calls=%async_computation.5 | async-start | bytes 1572864 | tf_op jit(solution)/shard_map/all_to_all | solution.py:211
  556.7 259.0 %collective-permute-start.6 = (bf16[3,8,128,128]{3,1,2,0:T(8,128)(2,1)}, bf16[3,8,128,128]{3,1,2,0:T(8,128)(2,1)}, u32[]{:S(2)}, u32[]{:S(2)}) collective-permute-start(bf16[3,8,128,128]{3,1,2,0:T(8,128)(2,1)} %get-tuple-element.267), channel_id=1, source_target_pairs={{8,0},{16,8},{24,16},{32,24},{40,32},{48,40},{56,48},{64,56},{72,6... | collective-permute-start | bytes 2359304 | tf_op jit(solution)/shard_map/ppermute | solution.py:20
  562.4 253.3 %collective-permute-start.7 = (bf16[3,8,128,128]{3,1,2,0:T(8,128)(2,1)}, bf16[3,8,128,128]{3,1,2,0:T(8,128)(2,1)}, u32[]{:S(2)}, u32[]{:S(2)}) collective-permute-start(bf16[3,8,128,128]{3,1,2,0:T(8,128)(2,1)} %get-tuple-element.268), channel_id=1, source_target_pairs={{0,8},{8,16},{16,24},{24,32},{32,40},{40,48},{48,56},{56,64},{64,7... | collective-permute-start | bytes 2359304 | tf_op jit(solution)/shard_map/ppermute | solution.py:20
  821.6 82.1 %all-to-all-start.7 = ((bf16[8,128,384]{1,2,0:T(8,128)(2,1)}), bf16[8,128,384]{1,2,0:T(8,128)(2,1)}, u32[]{:S(2)}, u32[]{:S(2)}) async-start(bf16[8,128,384]{1,2,0:T(8,128)(2,1)} %bitcast.242), calls=%async_computation.7 | async-start | bytes 1572864 | tf_op jit(solution)/shard_map/all_to_all | solution.py:213
  828.7 71.5 %collective-permute-start.4 = (bf16[3,8,128,128]{3,1,2,0:T(8,128)(2,1)}, bf16[3,8,128,128]{3,1,2,0:T(8,128)(2,1)S(1)}, u32[]{:S(2)}, u32[]{:S(2)}) collective-permute-start(bf16[3,8,128,128]{3,1,2,0:T(8,128)(2,1)} %get-tuple-element.269), channel_id=1, source_target_pairs={{8,0},{16,8},{24,16},{32,24},{40,32},{48,40},{56,48},{64,56},{72,6... | collective-permute-start | bytes 2359304 | tf_op jit(solution)/shard_map/ppermute | solution.py:20
  832.6 67.6 %collective-permute-start.5 = (bf16[3,8,128,128]{3,1,2,0:T(8,128)(2,1)}, bf16[3,8,128,128]{3,1,2,0:T(8,128)(2,1)S(1)}, u32[]{:S(2)}, u32[]{:S(2)}) collective-permute-start(bf16[3,8,128,128]{3,1,2,0:T(8,128)(2,1)} %get-tuple-element.270), channel_id=1, source_target_pairs={{0,8},{8,16},{16,24},{24,32},{32,40},{40,48},{48,56},{56,64},{64,7... | collective-permute-start | bytes 2359304 | tf_op jit(solution)/shard_map/ppermute | solution.py:20
  902.3 7.0 copy-start.6
  903.7 17.5 %all-to-all-start.6 = ((bf16[8,128,384]{1,2,0:T(8,128)(2,1)}), bf16[8,128,384]{1,2,0:T(8,128)(2,1)S(1)}, u32[]{:S(2)}, u32[]{:S(2)}) async-start(bf16[8,128,384]{1,2,0:T(8,128)(2,1)} %bitcast.76), calls=%async_computation.6 | async-start | bytes 1572864 | tf_op jit(solution)/shard_map/all_to_all | solution.py:212
Sparse Core Ops, SparseCore 0:
  60.5 282.0 all-reduce.5
  527.3 288.3 all-reduce.3
  818.8 77.1 all-gather.2
